TPU v7x, 32 devices: a whole 2x2x4 slice. The times are simulated.
32 devices in a mesh: shard: 4 (over x, core), context: 4 (over z), tensor: 2 (over y).
Axes of the slice: x: 2, y: 2, z: 4, core: 2. Of those that a mesh axis runs over, the one named last changes fastest.
Arguments:
- layer_input: bfloat16 [4, 2048, 1024], P('shard', 'context'), may hold values from -5 to 5
- segment_ids: int32 [4, 2048], P('shard'), may hold values from 0 to 3, never falling along the last dimension, each value on 1 to 1024 neighbouring positions
- out_grad: bfloat16 [4, 2048, 1024], P('shard', ('context', 'tensor')), may hold values from -6 to 6
- attn_in: float32 [3, 1024, 1024], P(None, 'shard', 'tensor'), may hold values from -0.1875 to 0.1875
- attn_out: float32 [1024, 1024], P('tensor', 'shard'), may hold values from -0.75 to 0.75
- mlp_up: float32 [1024, 4096], P('shard', 'tensor'), may hold values from -0.1875 to 0.1875
- mlp_down: float32 [4096, 1024], P('tensor', 'shard'), may hold values from -0.09375 to 0.09375
- vectors: float32 [8, 1024], replicated, may hold values from -0.8 to 1.4, as said below
- up_bias: float32 [4096], replicated, may hold values from -0.8 to 0.8
- attn_in_moments: float32 [2, 3, 1024, 1024], P(None, None, 'shard', 'tensor'), may hold values from -1.44 to 1.44, as said below
- attn_out_moments: float32 [2, 1024, 1024], P(None, 'tensor', 'shard'), may hold values from -3.6 to 3.6, as said below
- mlp_up_moments: float32 [2, 1024, 4096], P(None, 'shard', 'tensor'), may hold values from -2.16 to 2.16, as said below
- mlp_down_moments: float32 [2, 4096, 1024], P(None, 'tensor', 'shard'), may hold values from -4.32 to 4.32, as said below
- vector_moments: float32 [2, 8, 1024], replicated, may hold values from -7.2 to 7.2, as said below
- up_bias_moments: float32 [2, 4096], replicated, may hold values from -2.16 to 2.16, as said below
Outputs:
- block_output: bfloat16 [4, 2048, 1024], P('shard', ('context', 'tensor'))
- input_grad: bfloat16 [4, 2048, 1024], P('shard', ('context', 'tensor'))
- attn_in_grad: float32 [3, 1024, 1024], P(None, 'shard', 'tensor')
- attn_out_grad: float32 [1024, 1024], P('tensor', 'shard')
- mlp_up_grad: float32 [1024, 4096], P('shard', 'tensor')
- mlp_down_grad: float32 [4096, 1024], P('tensor', 'shard')
- vectors_grad: float32 [8, 1024], replicated
- up_bias_grad: float32 [4096], replicated
- attn_in_new: float32 [3, 1024, 1024], P(None, 'shard', 'tensor')
- attn_out_new: float32 [1024, 1024], P('tensor', 'shard')
- mlp_up_new: float32 [1024, 4096], P('shard', 'tensor')
- mlp_down_new: float32 [4096, 1024], P('tensor', 'shard')
- vectors_new: float32 [8, 1024], replicated
- up_bias_new: float32 [4096], replicated
- attn_in_moments_new: float32 [2, 3, 1024, 1024], P(None, None, 'shard', 'tensor')
- attn_out_moments_new: float32 [2, 1024, 1024], P(None, 'tensor', 'shard')
- mlp_up_moments_new: float32 [2, 1024, 4096], P(None, 'shard', 'tensor')
- mlp_down_moments_new: float32 [2, 4096, 1024], P(None, 'tensor', 'shard')
- vector_moments_new: float32 [2, 8, 1024], replicated
- up_bias_moments_new: float32 [2, 4096], replicated
Inputs may be any that keep to these rules, and one draw needn't show every extreme that they name: `vectors`: rows 4 and 6 are gains near one, the others biases near zero. `attn_in_moments`: index 0 holds first moments, index 1 positive second moments. `attn_out_moments`: index 0 holds first moments, index 1 positive second moments. `mlp_up_moments`: index 0 holds first moments, index 1 positive second moments. `mlp_down_moments`: index 0 holds first moments, index 1 positive second moments. `vector_moments`: index 0 holds first moments, index 1 positive second moments. `up_bias_moments`: index 0 holds first moments, index 1 positive second moments.
All inputs are finite; a program needn't handle non-finite values.
Results may differ from a plain program's by a relative error of at most 0.023.
Values may be sent and summed in bfloat16 or wider, within the bound.
No kernel may reach another device: no remote copies, remote signals or barrier semaphores. Data moves between devices by JAX's collectives and lax.ppermute only.
A program may use at most 256 MiB of HBM per device.

v0:
```python
import jax
import jax.numpy as jnp
from jax import lax
from jax.sharding import PartitionSpec as P

HD = 64
layer_eps = 1e-05
beta_one = 0.9
beta_two = 0.999
adam_eps = 1e-06
learning_rate = 0.02
weight_decay = 0.01
adam_step = 3.0
masked_score = -1e30


def normalize(hidden):
    center = hidden - jnp.mean(hidden, axis=-1, keepdims=True)
    scale = lax.rsqrt(jnp.mean(center * center, axis=-1, keepdims=True) + layer_eps)
    return (center * scale, scale)


def norm_back(upstream, normed, scale, gain):
    scaled = upstream * gain
    return scale * (
        scaled
        - jnp.mean(scaled, axis=-1, keepdims=True)
        - normed * jnp.mean(scaled * normed, axis=-1, keepdims=True)
    )


def gelu_value(value):
    return 0.5 * value * (1.0 + jax.scipy.special.erf(value * 0.7071067811865476))


def gelu_slope(value):
    return (
        0.5 * (1.0 + jax.scipy.special.erf(value * 0.7071067811865476))
        + value * jnp.exp(-0.5 * value * value) * 0.3989422804014327
    )


def adamw(param, moments, grad, decay):
    first = beta_one * moments[0] + (1.0 - beta_one) * grad
    second = beta_two * moments[1] + (1.0 - beta_two) * grad * grad
    update = (
        first
        / (1.0 - beta_one**adam_step)
        / (jnp.sqrt(second / (1.0 - beta_two**adam_step)) + adam_eps)
    )
    return (param - learning_rate * (update + decay * param), jnp.stack([first, second]))


def inner_rows(left, right):
    return lax.dot_general(
        left, right, (((0,), (0,)), ((), ())), preferred_element_type=jnp.float32
    )


def against_rows(left, right):
    return lax.dot_general(
        left, right, (((1,), (1,)), ((), ())), preferred_element_type=jnp.float32
    )


def over_context(grads):
    return (
        lax.psum(grads[0].astype(jnp.bfloat16), "context").astype(jnp.float32),
        lax.psum(grads[1].astype(jnp.bfloat16), "context").astype(jnp.float32),
        lax.psum(grads[2].astype(jnp.bfloat16), "context").astype(jnp.float32),
        lax.psum(grads[3].astype(jnp.bfloat16), "context").astype(jnp.float32),
    )


def to_owner(grads):
    return (
        lax.psum_scatter(
            grads[0].astype(jnp.bfloat16), "shard", scatter_dimension=1, tiled=True
        ).astype(jnp.float32),
        lax.psum_scatter(
            grads[1].astype(jnp.bfloat16), "shard", scatter_dimension=1, tiled=True
        ).astype(jnp.float32),
        lax.psum_scatter(
            grads[2].astype(jnp.bfloat16), "shard", scatter_dimension=0, tiled=True
        ).astype(jnp.float32),
        lax.psum_scatter(
            grads[3].astype(jnp.bfloat16), "shard", scatter_dimension=1, tiled=True
        ).astype(jnp.float32),
    )


def on_device(
    layer_input,
    segment_ids,
    out_grad,
    attn_in,
    attn_out,
    mlp_up,
    mlp_down,
    vectors,
    up_bias,
    attn_in_moments,
    attn_out_moments,
    mlp_up_moments,
    mlp_down_moments,
    vector_moments,
    up_bias_moments,
):
    tensor_count = lax.axis_size("tensor")
    tensor_rank = lax.axis_index("tensor")
    context_rank = lax.axis_index("context")
    seq_count = layer_input.shape[0]
    count_rows = layer_input.shape[1]
    model_width = vectors.shape[1]
    tokens = jnp.transpose(layer_input, (1, 0, 2)).reshape(count_rows * seq_count, model_width)
    all_rows = count_rows * seq_count
    share_tok = count_rows // tensor_count
    share_rows = share_tok * seq_count
    head_width = attn_in.shape[2]
    hidden_width = mlp_up.shape[1]
    length = segment_ids.shape[1]
    head_count = head_width // HD
    scale = 1.0 / HD**0.5
    in_full, out_full, up_full, down_full = (
        lax.all_gather(attn_in.astype(jnp.bfloat16), "shard", axis=1, tiled=True),
        lax.all_gather(attn_out.astype(jnp.bfloat16), "shard", axis=1, tiled=True),
        lax.all_gather(mlp_up.astype(jnp.bfloat16), "shard", axis=0, tiled=True),
        lax.all_gather(mlp_down.astype(jnp.bfloat16), "shard", axis=1, tiled=True),
    )
    head_start = tensor_rank * head_width
    unit_start = tensor_rank * hidden_width
    query_bias = lax.dynamic_slice_in_dim(vectors[0], head_start, head_width)
    value_bias = lax.dynamic_slice_in_dim(vectors[1], head_start, head_width)
    unit_bias = lax.dynamic_slice_in_dim(up_bias, unit_start, hidden_width)
    project = jnp.einsum("td,kdh->kth", tokens, in_full, preferred_element_type=jnp.float32)
    query_half = (project[0] + query_bias).astype(jnp.bfloat16)
    key_half = project[1].astype(jnp.bfloat16).reshape(count_rows, seq_count, head_width)
    value_half = (
        (project[2] + value_bias).astype(jnp.bfloat16).reshape(count_rows, seq_count, head_width)
    )
    keys_all, values_all = (
        lax.all_gather(key_half, "context", axis=0, tiled=True),
        lax.all_gather(value_half, "context", axis=0, tiled=True),
    )
    query_seq = query_half.reshape(count_rows, seq_count, head_count, HD)
    block = min(512, count_rows)
    blocks = count_rows // block

    def scores_of(which, lower):
        key_heads = keys_all[:, which].reshape(length, head_count, HD)
        segment = segment_ids[which]
        own_segment = lax.dynamic_slice_in_dim(segment, context_rank * count_rows, count_rows)
        raw = (
            jnp.einsum(
                "qhd,khd->hqk",
                query_seq[lower : lower + block, which],
                key_heads,
                preferred_element_type=jnp.float32,
            )
            * scale
        )
        same = own_segment[:, None] == segment[None, :]
        return jnp.where(same[None], raw, masked_score)

    which = 0
    value_heads = values_all[:, which].reshape(length, head_count, HD)
    parts = []
    index = 0
    raw = scores_of(which, index * block)
    top = jnp.max(raw, axis=-1, keepdims=True)
    total = top + jnp.log(jnp.sum(jnp.exp(raw - top), axis=-1, keepdims=True))
    attend = jnp.exp(raw - total).astype(jnp.bfloat16)
    parts.append(
        jnp.einsum("hqk,khd->qhd", attend, value_heads, preferred_element_type=jnp.float32).reshape(
            block, head_width
        )
    )
    totals = [total]
    seq_contexts = [parts[0]]
    context = jnp.stack(seq_contexts, 1).reshape(all_rows, head_width)
    context_half = context.astype(jnp.bfloat16)
    my_start = tensor_rank * share_rows
    attn_share = lax.psum_scatter(
        jnp.dot(context_half, out_full, preferred_element_type=jnp.float32).astype(jnp.bfloat16),
        "tensor",
        scatter_dimension=0,
        tiled=True,
    ).astype(jnp.float32)
    residual_in = lax.dynamic_slice_in_dim(tokens, my_start, share_rows, 0).astype(jnp.float32)
    normed_one, scale_one = normalize(residual_in + attn_share + vectors[2])
    first = normed_one * vectors[4] + vectors[5]
    first_all = lax.all_gather(first.astype(jnp.bfloat16), "tensor", axis=0, tiled=True)
    before = jnp.dot(first_all, up_full, preferred_element_type=jnp.float32) + unit_bias
    hidden_half = gelu_value(before).astype(jnp.bfloat16)
    mlp_share = lax.psum_scatter(
        jnp.dot(hidden_half, down_full, preferred_element_type=jnp.float32).astype(jnp.bfloat16),
        "tensor",
        scatter_dimension=0,
        tiled=True,
    ).astype(jnp.float32)
    normed_two, scale_two = normalize(first + mlp_share + vectors[3])
    block_output = (normed_two * vectors[6] + vectors[7]).astype(jnp.bfloat16)
    upstream = (
        jnp.transpose(out_grad, (1, 0, 2)).reshape(share_rows, model_width).astype(jnp.float32)
    )
    grad_two = norm_back(upstream, normed_two, scale_two, vectors[6])
    grad_two_all = lax.all_gather(grad_two.astype(jnp.bfloat16), "tensor", axis=0, tiled=True)
    down_grad = inner_rows(hidden_half, grad_two_all)
    grad_before = against_rows(grad_two_all, down_full) * gelu_slope(before)
    grad_before_half = grad_before.astype(jnp.bfloat16)
    up_grad = inner_rows(first_all, grad_before_half)
    grad_first = grad_two + lax.psum_scatter(
        against_rows(grad_before_half, up_full).astype(jnp.bfloat16),
        "tensor",
        scatter_dimension=0,
        tiled=True,
    ).astype(jnp.float32)
    grad_one = norm_back(grad_first, normed_one, scale_one, vectors[4])
    grad_one_all = lax.all_gather(grad_one.astype(jnp.bfloat16), "tensor", axis=0, tiled=True)
    out_grad_w = inner_rows(context_half, grad_one_all)
    grad_context = against_rows(grad_one_all, out_full).astype(jnp.bfloat16)
    grad_seq = grad_context.reshape(count_rows, seq_count, head_count, HD)
    delta = jnp.sum(
        grad_seq.astype(jnp.float32) * context.reshape(count_rows, seq_count, head_count, HD),
        axis=-1,
    )
    which = 0
    key_heads = keys_all[:, which].reshape(length, head_count, HD)
    value_heads = values_all[:, which].reshape(length, head_count, HD)
    parts = []
    index = 0
    lower = index * block
    raw = scores_of(which, lower)
    attend_full = jnp.exp(raw - totals[which * blocks + index])
    attend = attend_full.astype(jnp.bfloat16)
    part = grad_seq[lower : lower + block, which]
    shift = jnp.transpose(delta[lower : lower + block, which])[:, :, None]
    grad_probs = jnp.einsum("qhd,khd->hqk", part, value_heads, preferred_element_type=jnp.float32)
    grad_score = (attend_full * (grad_probs - shift) * scale).astype(jnp.bfloat16)
    parts.append(
        jnp.einsum(
            "hqk,khd->qhd", grad_score, key_heads, preferred_element_type=jnp.float32
        ).reshape(block, head_width)
    )
    key_acc = jnp.einsum(
        "hqk,qhd->khd",
        grad_score,
        query_seq[lower : lower + block, which],
        preferred_element_type=jnp.float32,
    )
    value_acc = jnp.einsum("hqk,qhd->khd", attend, part, preferred_element_type=jnp.float32)
    query_list = [parts[0]]
    key_list = [key_acc.reshape(length, head_width)]
    value_list = [value_acc.reshape(length, head_width)]
    query_grad = jnp.stack(query_list, 1).reshape(all_rows, head_width)
    key_own, value_own = (
        lax.psum_scatter(
            jnp.stack(key_list, 1).astype(jnp.bfloat16), "context", scatter_dimension=0, tiled=True
        ).astype(jnp.float32),
        lax.psum_scatter(
            jnp.stack(value_list, 1).astype(jnp.bfloat16),
            "context",
            scatter_dimension=0,
            tiled=True,
        ).astype(jnp.float32),
    )
    key_own = key_own.reshape(all_rows, head_width)
    value_own = value_own.reshape(all_rows, head_width)
    stacked = jnp.stack([query_grad, key_own, value_own]).astype(jnp.bfloat16)
    in_grad = jnp.einsum("td,kth->kdh", tokens, stacked, preferred_element_type=jnp.float32)
    input_share = grad_one + lax.psum_scatter(
        jnp.einsum("kth,kdh->td", stacked, in_full, preferred_element_type=jnp.float32).astype(
            jnp.bfloat16
        ),
        "tensor",
        scatter_dimension=0,
        tiled=True,
    ).astype(jnp.float32)
    input_grad = jnp.transpose(
        input_share.astype(jnp.bfloat16).reshape(share_tok, seq_count, model_width), (1, 0, 2)
    )
    output_block = jnp.transpose(block_output.reshape(share_tok, seq_count, model_width), (1, 0, 2))
    query_row = lax.dynamic_update_slice(
        jnp.zeros((model_width,), jnp.float32), jnp.sum(query_grad, 0), (head_start,)
    )
    value_row = lax.dynamic_update_slice(
        jnp.zeros((model_width,), jnp.float32), jnp.sum(value_own, 0), (head_start,)
    )
    local_vectors = jnp.stack(
        [
            query_row,
            value_row,
            jnp.sum(grad_one, 0),
            jnp.sum(grad_two, 0),
            jnp.sum(grad_first * normed_one, 0),
            jnp.sum(grad_first, 0),
            jnp.sum(upstream * normed_two, 0),
            jnp.sum(upstream, 0),
        ]
    )
    local_bias = lax.dynamic_update_slice(
        jnp.zeros((up_bias.shape[0],), jnp.float32), jnp.sum(grad_before, 0), (unit_start,)
    )
    vector_grad, bias_grad = lax.psum((local_vectors, local_bias), ("shard", "context", "tensor"))
    local_grads = (in_grad, out_grad_w, up_grad, down_grad)
    owned = to_owner(over_context(local_grads))
    in_sum, out_sum, up_sum, down_sum = owned
    in_new, in_moments = adamw(attn_in, attn_in_moments, in_sum, weight_decay)
    out_new, out_moments = adamw(attn_out, attn_out_moments, out_sum, weight_decay)
    up_new, up_moments = adamw(mlp_up, mlp_up_moments, up_sum, weight_decay)
    down_new, down_moments = adamw(mlp_down, mlp_down_moments, down_sum, weight_decay)
    vec_new, vec_moments = adamw(vectors, vector_moments, vector_grad, 0.0)
    bias_new, bias_moments = adamw(up_bias, up_bias_moments, bias_grad, 0.0)
    return (
        output_block,
        input_grad,
        in_sum,
        out_sum,
        up_sum,
        down_sum,
        vector_grad,
        bias_grad,
        in_new,
        out_new,
        up_new,
        down_new,
        vec_new,
        bias_new,
        in_moments,
        out_moments,
        up_moments,
        down_moments,
        vec_moments,
        bias_moments,
    )


def solution(mesh):
    in_specs = (
        P("shard", "context", None),
        P("shard", None),
        P("shard", ("context", "tensor"), None),
        P(None, "shard", "tensor"),
        P("tensor", "shard"),
        P("shard", "tensor"),
        P("tensor", "shard"),
        P(),
        P(),
        P(None, None, "shard", "tensor"),
        P(None, "tensor", "shard"),
        P(None, "shard", "tensor"),
        P(None, "tensor", "shard"),
        P(),
        P(),
    )
    out_specs = (
        P("shard", ("context", "tensor"), None),
        P("shard", ("context", "tensor"), None),
        P(None, "shard", "tensor"),
        P("tensor", "shard"),
        P("shard", "tensor"),
        P("tensor", "shard"),
        P(),
        P(),
        P(None, "shard", "tensor"),
        P("tensor", "shard"),
        P("shard", "tensor"),
        P("tensor", "shard"),
        P(),
        P(),
        P(None, None, "shard", "tensor"),
        P(None, "tensor", "shard"),
        P(None, "shard", "tensor"),
        P(None, "tensor", "shard"),
        P(),
        P(),
    )
    return jax.shard_map(
        on_device, mesh=mesh, in_specs=in_specs, out_specs=out_specs, check_vma=False
    )
```

profile of v0, /device:TPU:0, one launch (start us, length us, event | category | flops | bytes accessed | tf_op | source)
XLA Modules:
  0.0 855.1 jit_solution(14302809599329487599)
XLA Ops:
  7.2 1.9 copy.35
  10.2 31.7 %all-gather.11.cloned.1.call-done = bf16[3,1024,512]{1,2,0:T(8,128)(2,1)} async-done(((bf16[3,256,512]{1,2,0:T(8,128)(2,1)}), bf16[3,1024,512]{1,2,0:T(8,128)(2,1)}) %all-gather.11.cloned.1.call-update) | async-done | bytes 3145744 | tf_op jit(solution)/shard_map/all_gather | solution.py:125
  41.9 3.7 convolution_bitcast_fusion
  45.7 1.7 copy-done.24
  48.3 2.2 fusion.20
  52.4 2.3 slice.96
  54.6 39.4 %all-gather.27.cloned.1.call-done = bf16[1,2048,512]{1,2,0:T(8,128)(2,1)} async-done(((bf16[1,512,512]{1,2,0:T(8,128)(2,1)}), bf16[1,2048,512]{1,2,0:T(8,128)(2,1)}) %all-gather.27.cloned.1.call-update) | async-done | bytes 2097168 | tf_op jit(solution)/shard_map/all_gather | solution.py:142
  94.0 16.0 %fusion.1 = (f32[8,512]{1,0:T(8,128)S(1)}, f32[8,512,2048]{2,1,0:T(8,128)}) fusion(pred[512,2048]{1,0:T(8,128)(4,1)S(1)} %broadcast_compare_fusion, bf16[2048,8,64]{0,2,1:T(8,128)(2,1)} %bitcast.208, f32[512,8,64]{0,2,1:T(8,128)} %bitcast.9, f32[8,64]{1,0:T(8,128)S(1)} %add.261), kind=kOutput, calls=%fused_computation.5 | convolution fusion | flops 1099427840 | bytes 37767168 | tf_op jit(solution)/shard_map/qhd,khd->hqk/dot_general | solution.py:154
  110.0 15.1 %exponential_reduce_fusion = f32[8,512]{1,0:T(8,128)S(1)} fusion(f32[8,512,2048]{2,1,0:T(8,128)} %get-tuple-element.97, f32[8,512]{1,0:T(8,128)S(1)} %get-tuple-element.96, pred[512,2048]{1,0:T(8,128)(4,1)S(1)} %broadcast_compare_fusion), kind=kLoop, calls=%fused_computation.2 | loop fusion | flops 33550336 | bytes 34635776 | tf_op jit(solution)/shard_map/reduce_sum | solution.py:171
  125.2 15.5 %all-gather.13.cloned.1.call-done = bf16[2048,1,512]{0,2,1:T(8,128)(2,1)} async-done(((bf16[512,1,512]{0,2,1:T(8,128)(2,1)}), bf16[2048,1,512]{0,2,1:T(8,128)(2,1)}) %all-gather.13.cloned.1.call-update) | async-done | bytes 2097168 | tf_op jit(solution)/shard_map/all_gather | solution.py:143
  140.7 16.4 %fusion.57 = (bf16[512,8,64]{0,2,1:T(8,128)(2,1)S(1)}, f32[512,8,64]{0,2,1:T(8,128)}) fusion(bf16[2048,8,64]{0,2,1:T(8,128)(2,1)} %bitcast.248, f32[8,512,2048]{2,1,0:T(8,128)} %get-tuple-element.97, f32[8,512]{1,0:T(8,128)S(1)} %log_add_fusion, pred[512,2048]{1,0:T(8,128)(4,1)S(1)} %broadcast_compare_fusion), kind=kOutput, calls=%fused_computation.137 | convolution fusion | flops 1107558400 | bytes 38289408 | tf_op jit(solution)/shard_map/hqk,khd->qhd/dot_general | solution.py:174
  158.3 2.9 convolution_convert_fusion.5
  161.3 2.8 convert_element_type.201
  164.2 17.6 %reduce-scatter.11.cloned.1.call-done = bf16[256,1024]{1,0:T(8,128)(2,1)} async-done(((bf16[512,1024]{1,0:T(8,128)(2,1)}), bf16[256,1024]{1,0:T(8,128)(2,1)}) %reduce-scatter.11.cloned.1.call-update) | async-done | bytes 524304 | tf_op jit(solution)/shard_map/reduce_scatter | solution.py:183
  181.8 1.4 fusion.27
  183.2 1.4 multiply_reduce_fusion.4
  185.8 2.7 convert_element_type.203
  188.9 29.4 %all-gather.19.cloned.1.call-done = bf16[1024,2048]{1,0:T(8,128)(2,1)} async-done(((bf16[256,2048]{1,0:T(8,128)(2,1)}), bf16[1024,2048]{1,0:T(8,128)(2,1)}) %all-gather.19.cloned.1.call-update) | async-done | bytes 4194320 | tf_op jit(solution)/shard_map/all_gather | solution.py:127
  218.3 23.4 %all-gather.17.cloned.1.call-done = bf16[512,1024]{1,0:T(8,128)(2,1)} async-done(((bf16[256,1024]{1,0:T(8,128)(2,1)}), bf16[512,1024]{1,0:T(8,128)(2,1)}) %all-gather.17.cloned.1.call-update) | async-done | bytes 1048592 | tf_op jit(solution)/shard_map/all_gather | solution.py:192
  241.7 7.9 multiply_convert_fusion.1
  249.6 29.3 %all-gather.21.cloned.1.call-done = bf16[2048,1024]{1,0:T(8,128)(2,1)} async-done(((bf16[2048,256]{1,0:T(8,128)(2,1)}), bf16[2048,1024]{1,0:T(8,128)(2,1)}) %all-gather.21.cloned.1.call-update) | async-done | bytes 4194320 | tf_op jit(solution)/shard_map/all_gather | solution.py:128
  278.9 6.1 convolution_convert_fusion.7
  285.1 20.5 %reduce-scatter.13.cloned.1.call-done = bf16[256,1024]{1,0:T(8,128)(2,1)} async-done(((bf16[512,1024]{1,0:T(8,128)(2,1)}), bf16[256,1024]{1,0:T(8,128)(2,1)}) %reduce-scatter.13.cloned.1.call-update) | async-done | bytes 524304 | tf_op jit(solution)/shard_map/reduce_scatter | solution.py:195
  305.6 1.8 fusion.53
  308.2 1.8 fusion.51
  310.0 21.4 %all-gather.23.cloned.1.call-done = bf16[512,1024]{1,0:T(8,128)(2,1)} async-done(((bf16[256,1024]{1,0:T(8,128)(2,1)}), bf16[512,1024]{1,0:T(8,128)(2,1)}) %all-gather.23.cloned.1.call-update) | async-done | bytes 1048592 | tf_op jit(solution)/shard_map/all_gather | solution.py:207
  331.4 7.1 fusion.58
  339.8 3.3 convolution_convert_fusion.6
  343.2 20.5 %reduce-scatter.15.cloned.1.call-done = bf16[256,1024]{1,0:T(8,128)(2,1)} async-done(((bf16[512,1024]{1,0:T(8,128)(2,1)}), bf16[256,1024]{1,0:T(8,128)(2,1)}) %reduce-scatter.15.cloned.1.call-update) | async-done | bytes 524304 | tf_op jit(solution)/shard_map/reduce_scatter | solution.py:212
  363.7 2.8 multiply_reduce_fusion
  369.8 21.2 %all-gather.25.cloned.1.call-done = bf16[512,1024]{1,0:T(8,128)(2,1)} async-done(((bf16[256,1024]{1,0:T(8,128)(2,1)}), bf16[512,1024]{1,0:T(8,128)(2,1)}) %all-gather.25.cloned.1.call-update) | async-done | bytes 1048592 | tf_op jit(solution)/shard_map/all_gather | solution.py:219
  391.0 3.4 multiply_reduce_fusion.1
  394.3 15.3 %convolution_convert_fusion.2 = bf16[8,64,2048]{2,1,0:T(8,128)(2,1)S(1)} fusion(bf16[512,8,64]{0,2,1:T(8,128)(2,1)} %bitcast.213, f32[8,512,2048]{2,1,0:T(8,128)} %get-tuple-element.97, f32[8,512]{1,0:T(8,128)S(1)} %log_add_fusion, pred[512,2048]{1,0:T(8,128)(4,1)S(1)} %broadcast_compare_fusion), kind=kOutput, calls=%fused_computation.22 | convolution fusion | flops 1108344832 | bytes 37240832 | tf_op jit(solution)/shard_map/hqk,qhd->khd/dot_general | solution.py:251
  409.6 2.5 copy.37
  412.2 17.9 %multiply_convert_fusion = bf16[8,512,2048]{2,1,0:T(8,128)(2,1)S(1)} fusion(f32[8,512,2048]{2,1,0:T(8,128)} %get-tuple-element.97, bf16[512,8,64]{0,2,1:T(8,128)(2,1)} %bitcast.214, bf16[2048,8,64]{0,2,1:T(8,128)(2,1)} %bitcast.249, f32[8,512]{1,0:T(8,128)} %bitcast.235, f32[8,512]{1,0:T(8,128)} %copy-done.46, pred[512,2048]{1,0:T(8,128)(4,1)S(1)} %broadcast_compare_fusion), kind=kOutput, calls=%fused_computation | convolution fusion | flops 1132462080 | bytes 54034432 | tf_op jit(solution)/shard_map/qhd,khd->hqk/dot_general | solution.py:238
  430.2 6.8 convolution_convert_fusion.3
  437.0 3.9 copy.36
  442.3 1.7 convolution_convert_fusion.4
  444.3 6.0 convolution_convert_fusion
  452.2 4.4 convolution_convert_fusion.1
  456.7 1.5 copy-done.4
  458.2 11.8 %fusion.55 = (f32[8,64]{1,0:T(8,128)S(1)}, bf16[512,8,64]{0,2,1:T(8,128)(2,1)}) fusion(bf16[2048,8,64]{0,2,1:T(8,128)(2,1)S(1)} %bitcast.209, bf16[8,512,2048]{2,1,0:T(8,128)(2,1)} %copy-done), kind=kOutput, calls=%fused_computation.135 | convolution fusion | flops 1074265600 | bytes 19400704 | tf_op jit(solution)/shard_map/hqk,khd->qhd/dot_general | solution.py:241
  471.3 30.2 %reduce-scatter.17.cloned.1.call-done = bf16[512,1,512]{2,0,1:T(8,128)(2,1)} async-done(((bf16[2048,1,512]{2,0,1:T(8,128)(2,1)}), bf16[512,1,512]{2,0,1:T(8,128)(2,1)}) %reduce-scatter.17.cloned.1.call-update) | async-done | bytes 524304 | tf_op jit(solution)/shard_map/reduce_scatter | solution.py:257
  501.5 4.7 convert_bitcast_fusion
  507.4 4.8 bitcast_convert_fusion
  512.6 15.9 %reduce-scatter.25.cloned.1.call-done = bf16[512,256]{1,0:T(8,128)(2,1)} async-done(((bf16[512,1024]{1,0:T(8,128)(2,1)}), bf16[512,256]{1,0:T(8,128)(2,1)}) %reduce-scatter.25.cloned.1.call-update) | async-done | bytes 262160 | tf_op jit(solution)/shard_map/reduce_scatter | solution.py:80
  528.5 47.4 %reduce-scatter.29.cloned.1.call-done = bf16[2048,256]{1,0:T(8,128)(2,1)} async-done(((bf16[2048,1024]{1,0:T(8,128)(2,1)}), bf16[2048,256]{1,0:T(8,128)(2,1)}) %reduce-scatter.29.cloned.1.call-update) | async-done | bytes 1048592 | tf_op jit(solution)/shard_map/reduce_scatter | solution.py:86
  575.9 47.6 %reduce-scatter.27.cloned.1.call-done = bf16[256,2048]{1,0:T(8,128)(2,1)} async-done(((bf16[1024,2048]{1,0:T(8,128)(2,1)}), bf16[256,2048]{1,0:T(8,128)(2,1)}) %reduce-scatter.27.cloned.1.call-update) | async-done | bytes 1048592 | tf_op jit(solution)/shard_map/reduce_scatter | solution.py:83
  623.4 40.7 %reduce-scatter.23.cloned.1.call-done = bf16[3,256,512]{1,2,0:T(8,128)(2,1)} async-done(((bf16[3,1024,512]{1,2,0:T(8,128)(2,1)}), bf16[3,256,512]{1,2,0:T(8,128)(2,1)}) %reduce-scatter.23.cloned.1.call-update) | async-done | bytes 786448 | tf_op jit(solution)/shard_map/reduce_scatter | solution.py:77
  664.2 3.5 fusion.54
  668.2 3.1 copy.51
  673.3 41.5 %all-reduce = (f32[8,1024]{1,0:T(8,128)S(1)}, f32[4096]{0:T(1024)S(1)}) all-reduce(f32[8,1024]{1,0:T(8,128)S(1)} %stack.97, f32[4096]{0:T(1024)S(1)} %dynamic_update_slice.13), channel_id=1, replica_groups=mesh['shard'=4,'context'=4,'tensor'=2] {'shard','context','tensor'}, use_global_device_ids=true, to_apply=%region_33.34 | all-reduce | flops 12288 | bytes 98304 | tf_op jit(solution)/shard_map/psum | solution.py:304
  717.4 2.0 fusion.34
  719.4 92.5 %all-reduce.4.cloned.1.call-done = (bf16[3,256,512]{1,2,0:T(8,128)(2,1)}, bf16[512,256]{1,0:T(8,128)(2,1)}, bf16[256,2048]{1,0:T(8,128)(2,1)}, bf16[2048,256]{1,0:T(8,128)(2,1)}) async-done(((bf16[3,256,512]{1,2,0:T(8,128)(2,1)}, bf16[512,256]{1,0:T(8,128)(2,1)}, bf16[256,2048]{1,0:T(8,128)(2,1)}, bf16[2048,256]{1,0:T(8,128)(2,1)}), (bf16[3,256,512]{1,2,0:T(8,128)(2,1)}, bf16[512,256]{1,0:T(8,128)(2,1)}, ...) | async-done | bytes 3145744 | tf_op jit(solution)/shard_map/psum | solution.py:68
  811.9 3.7 fusion.31
  816.5 3.6 fusion.35
  820.1 1.8 fusion.30
  822.1 3.6 fusion.36
  828.1 2.6 copy.45
  830.7 4.1 fusion.28
  834.9 2.4 copy.47
  837.3 3.2 copy.46
  840.5 4.0 pad_maximum_fusion.1
  844.5 2.3 pad_maximum_fusion
  (203 shorter events, 28.6 us)
Async XLA Ops:
  7.2 34.7 %all-gather.11.cloned.1.call-start = ((), (), s32[]{:S(2)}) async-start(), calls=%async_computation.10 | async-start | bytes 3932160 | tf_op jit(solution)/shard_map/all_gather | solution.py:125
  9.1 36.5 %copy-start.2 = (f32[3,256,512]{1,2,0:T(8,128)}, f32[3,256,512]{1,2,0:T(8,128)S(1)}, u32[]{:S(2)}) copy-start(f32[3,256,512]{1,2,0:T(8,128)S(1)} %copy.35) | copy-start | bytes 4718596
  9.1 32.8 %copy-start.7 = (bf16[1,512,1024]{2,1,0:T(8,128)(2,1)S(1)}, bf16[1,512,1024]{2,1,0:T(8,128)(2,1)}, u32[]{:S(2)}) copy-start(bf16[1,512,1024]{2,1,0:T(8,128)(2,1)} %param.15) | copy-start | bytes 3145732
  10.1 38.1 %copy-start.37 = (f32[8,1024]{1,0:T(8,128)S(1)}, f32[8,1024]{1,0:T(8,128)}, u32[]{:S(2)}) copy-start(f32[8,1024]{1,0:T(8,128)} %param.22) | copy-start | bytes 98308
  10.1 83.9 %all-gather.27.cloned.1.call-start = ((), (), s32[]{:S(2)}) async-start(), calls=%async_computation.24 | async-start | bytes 2621440 | tf_op jit(solution)/shard_map/all_gather | solution.py:142
  47.3 3.2 copy-start.27
  48.2 3.5 copy-start.49
  48.2 92.5 %all-gather.13.cloned.1.call-start = ((), (), s32[]{:S(2)}) async-start(), calls=%async_computation.11 | async-start | bytes 2621440 | tf_op jit(solution)/shard_map/all_gather | solution.py:143
  50.5 107.8 %all-gather.15.cloned.1.call-start = ((), (), s32[]{:S(2)}) async-start(), calls=%async_computation.12 | async-start | bytes 1310720 | tf_op jit(solution)/shard_map/all_gather | solution.py:126
  51.3 130.5 %reduce-scatter.11.cloned.1.call-start = ((), (), s32[]{:S(2)}) async-start(), calls=%async_computation.13 | async-start | bytes 1572864 | tf_op jit(solution)/shard_map/reduce_scatter | solution.py:183
  125.2 269.2 %copy-start.46 = (f32[8,512]{1,0:T(8,128)}, f32[8,512]{1,0:T(8,128)S(1)}, u32[]{:S(2)}) copy-start(f32[8,512]{1,0:T(8,128)S(1)} %log_add_fusion) | copy-start | bytes 49156
  157.1 7.0 copy-start.55
  161.3 20.5 %copy-start.8 = (bf16[1,512,1024]{2,1,0:T(8,128)(2,1)S(1)}, bf16[1,512,1024]{2,1,0:T(8,128)(2,1)}, u32[]{:S(2)}) copy-start(bf16[1,512,1024]{2,1,0:T(8,128)(2,1)} %param.15) | copy-start | bytes 3145732
  161.3 57.0 %all-gather.19.cloned.1.call-start = ((), (), s32[]{:S(2)}) async-start(), calls=%async_computation.15 | async-start | bytes 5242880 | tf_op jit(solution)/shard_map/all_gather | solution.py:127
  164.1 77.6 %all-gather.17.cloned.1.call-start = ((), (), s32[]{:S(2)}) async-start(), calls=%async_computation.14 | async-start | bytes 1572864 | tf_op jit(solution)/shard_map/all_gather | solution.py:192
  181.8 2.8 copy-start.1
  185.7 3.2 copy-start.40
  185.7 93.2 %all-gather.21.cloned.1.call-start = ((), (), s32[]{:S(2)}) async-start(), calls=%async_computation.16 | async-start | bytes 5242880 | tf_op jit(solution)/shard_map/all_gather | solution.py:128
  188.4 117.1 %reduce-scatter.13.cloned.1.call-start = ((), (), s32[]{:S(2)}) async-start(), calls=%async_computation.17 | async-start | bytes 1572864 | tf_op jit(solution)/shard_map/reduce_scatter | solution.py:195
  285.0 22.6 %copy-start.21 = (bf16[1,256,1024]{2,1,0:T(8,128)(2,1)S(1)}, bf16[1,256,1024]{2,1,0:T(8,128)(2,1)}, u32[]{:S(2)}) copy-start(bf16[1,256,1024]{2,1,0:T(8,128)(2,1)} %param.17) | copy-start | bytes 1572868
  285.0 46.3 %all-gather.23.cloned.1.call-start = ((), (), s32[]{:S(2)}) async-start(), calls=%async_computation.18 | async-start | bytes 1572864 | tf_op jit(solution)/shard_map/all_gather | solution.py:207
  310.0 53.8 %reduce-scatter.15.cloned.1.call-start = ((), (), s32[]{:S(2)}) async-start(), calls=%async_computation.19 | async-start | bytes 1572864 | tf_op jit(solution)/shard_map/reduce_scatter | solution.py:212
  331.4 8.4 copy-start.51
  339.8 23.9 %copy-start.9 = (bf16[1,512,1024]{2,1,0:T(8,128)(2,1)S(1)}, bf16[1,512,1024]{2,1,0:T(8,128)(2,1)}, u32[]{:S(2)}) copy-start(bf16[1,512,1024]{2,1,0:T(8,128)(2,1)} %param.15) | copy-start | bytes 3145732
  343.1 47.8 %all-gather.25.cloned.1.call-start = ((), (), s32[]{:S(2)}) async-start(), calls=%async_computation.20 | async-start | bytes 1572864 | tf_op jit(solution)/shard_map/all_gather | solution.py:219
  363.7 2.9 copy-start.13
  363.7 2.9 copy-start.30
  367.7 23.3 %copy-start.31 = (bf16[512,1024]{1,0:T(8,128)(2,1)S(1)}, bf16[512,1024]{1,0:T(8,128)(2,1)}, u32[]{:S(2)}) copy-start(bf16[512,1024]{1,0:T(8,128)(2,1)} %all-gather.15.cloned.1.call-done) | copy-start | bytes 3145732
  367.7 23.3 %copy-start.32 = (f32[512,8,64]{0,2,1:T(8,128)S(1)}, f32[512,8,64]{0,2,1:T(8,128)}, u32[]{:S(2)}) copy-start(f32[512,8,64]{0,2,1:T(8,128)} %get-tuple-element.99) | copy-start | bytes 3145732
  369.5 101.7 %reduce-scatter.19.cloned.1.call-start = ((), (), s32[]{:S(2)}) async-start(), calls=%async_computation.22 | async-start | bytes 2621440 | tf_op jit(solution)/shard_map/reduce_scatter | solution.py:260
  412.2 89.4 %reduce-scatter.17.cloned.1.call-start = ((), (), s32[]{:S(2)}) async-start(), calls=%async_computation.21 | async-start | bytes 2621440 | tf_op jit(solution)/shard_map/reduce_scatter | solution.py:257
  430.2 6.8 copy-start
  441.0 3.3 copy-start.53
  441.0 87.5 %reduce-scatter.25.cloned.1.call-start = ((), (), s32[]{:S(2)}) async-start(), calls=%async_computation.26 | async-start | bytes 1310720 | tf_op jit(solution)/shard_map/reduce_scatter | solution.py:80
  444.0 131.9 %reduce-scatter.29.cloned.1.call-start = ((), (), s32[]{:S(2)}) async-start(), calls=%async_computation.28 | async-start | bytes 5242880 | tf_op jit(solution)/shard_map/reduce_scatter | solution.py:86
  450.3 173.1 %reduce-scatter.27.cloned.1.call-start = ((), (), s32[]{:S(2)}) async-start(), calls=%async_computation.27 | async-start | bytes 5242880 | tf_op jit(solution)/shard_map/reduce_scatter | solution.py:83
  456.6 44.9 %copy-start.10 = (bf16[1,512,1024]{2,1,0:T(8,128)(2,1)S(1)}, bf16[1,512,1024]{2,1,0:T(8,128)(2,1)}, u32[]{:S(2)}) copy-start(bf16[1,512,1024]{2,1,0:T(8,128)(2,1)} %param.15) | copy-start | bytes 3145732
  456.6 207.5 %reduce-scatter.23.cloned.1.call-start = ((), (), s32[]{:S(2)}) async-start(), calls=%async_computation.25 | async-start | bytes 3932160 | tf_op jit(solution)/shard_map/reduce_scatter | solution.py:77
  506.3 211.1 %reduce-scatter.21.cloned.1.call-start = ((), (), s32[]{:S(2)}) async-start(), calls=%async_computation.23 | async-start | bytes 1572864 | tf_op jit(solution)/shard_map/reduce_scatter | solution.py:271
  512.3 299.7 %all-reduce.4.cloned.1.call-start = ((), (), s32[]{:S(2)}) async-start(), calls=%async_computation.29 | async-start | bytes 6291456 | tf_op jit(solution)/shard_map/psum | solution.py:68
  668.1 3.3 copy-start.22
  668.1 3.4 copy-start.43
  668.1 3.4 copy-start.50
  668.2 5.1 copy-start.44
  668.2 5.1 copy-start.45
  668.2 5.1 copy-start.48
  668.2 46.6 %copy-start.38 = (f32[8,1024]{1,0:T(8,128)S(1)}, f32[8,1024]{1,0:T(8,128)}, u32[]{:S(2)}) copy-start(f32[8,1024]{1,0:T(8,128)} %param.22) | copy-start | bytes 98308
  668.2 46.6 %copy-start.39 = (f32[2,8,1024]{2,1,0:T(8,128)S(1)}, f32[2,8,1024]{2,1,0:T(8,128)}, u32[]{:S(2)}) copy-start(f32[2,8,1024]{2,1,0:T(8,128)} %param.28) | copy-start | bytes 196612
  668.2 47.9 %copy-start.41 = (f32[4096]{0:T(1024)S(1)}, f32[4096]{0:T(1024)}, u32[]{:S(2)}) copy-start(f32[4096]{0:T(1024)} %param.23) | copy-start | bytes 49156
  668.2 49.2 %copy-start.12 = (f32[256,1024]{1,0:T(8,128)S(1)}, f32[256,1024]{1,0:T(8,128)}, u32[]{:S(2)}) copy-start(f32[256,1024]{1,0:T(8,128)} %copy-done.11) | copy-start | bytes 3145732
  714.8 100.8 %copy-start.42 = (f32[8,1024]{1,0:T(8,128)}, f32[8,1024]{1,0:T(8,128)S(1)}, u32[]{:S(2)}) copy-start(f32[8,1024]{1,0:T(8,128)S(1)} %get-tuple-element.48) | copy-start | bytes 98308
  714.8 100.8 %copy-start.47 = (f32[4096]{0:T(1024)}, f32[4096]{0:T(1024)S(1)}, u32[]{:S(2)}) copy-start(f32[4096]{0:T(1024)S(1)} %get-tuple-element.49) | copy-start | bytes 49156
  811.9 3.7 copy-start.5
  811.9 4.6 copy-start.18
  815.6 4.4 copy-start.14
  816.5 3.6 copy-start.6
  816.5 3.6 copy-start.33
  821.8 3.8 copy-start.15
  822.0 3.6 copy-start.23
  822.1 3.6 copy-start.36
  826.8 3.9 copy-start.3
  837.3 3.2 copy-start.16
  840.5 4.0 copy-start.17
  840.5 4.0 copy-start.20
  (15 other events, 22.9 us)
Sparse Core Ops, SparseCore 0:
  10.2 31.6 all-gather.10
  48.3 45.6 all-gather.26
  96.2 44.4 all-gather.12
  142.7 15.6 all-gather.14
  161.4 20.3 reduce-scatter.10
  183.8 34.4 all-gather.18
  220.4 21.2 all-gather.16
  243.8 34.9 all-gather.20
  285.1 20.3 reduce-scatter.12
  310.1 21.2 all-gather.22
  343.3 20.3 reduce-scatter.14
  369.7 21.2 all-gather.24
  412.3 43.6 reduce-scatter.18
  458.7 42.8 reduce-scatter.16
  504.5 23.9 reduce-scatter.24
  531.4 44.3 reduce-scatter.28
  578.8 44.5 reduce-scatter.26
  626.4 37.7 reduce-scatter.22
  667.0 20.9 reduce-scatter.20
  690.4 121.4 all-reduce.3
where the time goes:
time: 859 us; the launch traced here: 855 us
  waiting for transfers between devices  546 us (64%)
  matrix products  140 us (16%)
  other arithmetic  70.4 us (8%)
  blocking collectives  41.5 us (5%)
  local copies, waits for them, and re-layouts  39.8 us (5%)
  between operations  15.3 us (2%)
    psum x1, waiting for transfers between devices, over_context(): lax.psum(grads[0].astype(jnp.bfloat16), 'context').astype(jnp.float32)  92.5 us
    reduce_scatter x1, waiting for transfers between devices, to_owner(): lax.psum_scatter(grads[2].astype(jnp.bfloat16), 'shard', scatter_dimensio...  47.6 us
    reduce_scatter x1, waiting for transfers between devices, to_owner(): lax.psum_scatter(grads[3].astype(jnp.bfloat16), 'shard', scatter_dimensio...  47.4 us
    psum x1, blocking collectives, on_device(): lax.psum((local_vectors, local_bias), ('shard', 'context', 'tensor'))  41.5 us
    reduce_scatter x1, waiting for transfers between devices, to_owner(): lax.psum_scatter(grads[0].astype(jnp.bfloat16), 'shard', scatter_dimensio...  40.7 us
    all_gather x1, waiting for transfers between devices, on_device(): lax.all_gather(key_half, 'context', axis=0, tiled=True)  39.4 us
    all_gather x1, waiting for transfers between devices, on_device(): lax.all_gather(attn_in.astype(jnp.bfloat16), 'shard', axis=1, tiled=True)  31.7 us
    reduce_scatter x1, waiting for transfers between devices, on_device(): lax.psum_scatter(jnp.stack(key_list, 1).astype(jnp.bfloat16), 'context',...  30.2 us
  transfers between devices with their start and end apart: 20, of which 18 were waited for; matrix products, arithmetic and copies ran while one was open for 17% of the time, Pallas kernels for 0%

commit v1 on v0

--- a/solution.py
+++ b/solution.py
@@ -65,7 +65,9 @@
 
 def over_context(grads):
     return (
-        lax.psum(grads[0].astype(jnp.bfloat16), "context").astype(jnp.float32),
+        jnp.sum(lax.all_gather(grads[0].astype(jnp.bfloat16), "context"), axis=0).astype(
+            jnp.float32
+        ),
         lax.psum(grads[1].astype(jnp.bfloat16), "context").astype(jnp.float32),
         lax.psum(grads[2].astype(jnp.bfloat16), "context").astype(jnp.float32),
         lax.psum(grads[3].astype(jnp.bfloat16), "context").astype(jnp.float32),

time: 859 us -> 1030 us (1.20)
  waiting for transfers between devices: 546 us -> 703 us
    all_gather x0 -> x1, waiting for transfers between devices: none -> 214 us  [over_context(): lax.all_gather(grads[0].astype(jnp.bfloat16), 'context')]
    psum x1, waiting for transfers between devices: 92.5 us -> 61.3 us  [over_context(): lax.psum(grads[1].astype(jnp.bfloat16), 'context').astype(jnp.float32)]
    reduce_scatter x1, waiting for transfers between devices: 40.7 us -> 19.3 us  [to_owner(): lax.psum_scatter(grads[0].astype(jnp.bfloat16), 'shard', scatter_dimensio...]
    unnamed x124 -> x121, local copies, waits for them, and re-layouts: 24.8 us -> 30.5 us
  transfers between devices with their start and end apart: 20 -> 21, of which waited for: 18 -> 19; matrix products, arithmetic and copies ran while one was open for 17% -> 17% of each run, Pallas kernels for 0% -> 0%
where the time goes in v1:
time: 1030 us; the launch traced here: 1020 us
  waiting for transfers between devices  703 us (68%)
  matrix products  140 us (14%)
  other arithmetic  69.5 us (7%)
  local copies, waits for them, and re-layouts  48.9 us (5%)
  blocking collectives  42.3 us (4%)
  between operations  15.1 us (1%)
    all_gather x1, waiting for transfers between devices, over_context(): lax.all_gather(grads[0].astype(jnp.bfloat16), 'context')  214 us
    psum x1, waiting for transfers between devices, over_context(): lax.psum(grads[1].astype(jnp.bfloat16), 'context').astype(jnp.float32)  61.3 us
    reduce_scatter x1, waiting for transfers between devices, to_owner(): lax.psum_scatter(grads[2].astype(jnp.bfloat16), 'shard', scatter_dimensio...  47.6 us
    reduce_scatter x1, waiting for transfers between devices, to_owner(): lax.psum_scatter(grads[3].astype(jnp.bfloat16), 'shard', scatter_dimensio...  47.4 us
    psum x1, blocking collectives, on_device(): lax.psum((local_vectors, local_bias), ('shard', 'context', 'tensor'))  42.3 us
    all_gather x1, waiting for transfers between devices, on_device(): lax.all_gather(key_half, 'context', axis=0, tiled=True)  39.3 us
    all_gather x1, waiting for transfers between devices, on_device(): lax.all_gather(attn_in.astype(jnp.bfloat16), 'shard', axis=1, tiled=True)  31.7 us
    unnamed x121, local copies, waits for them, and re-layouts  30.5 us
  transfers between devices with their start and end apart: 21, of which 19 were waited for; matrix products, arithmetic and copies ran while one was open for 17% of the time, Pallas kernels for 0%

profile of v1, /device:TPU:0, one launch (start us, length us, event | category | flops | bytes accessed | tf_op | source)
XLA Modules:
  0.0 1021.2 jit_solution(17655979971790409259)
XLA Ops:
  7.2 1.9 copy.41
  10.2 31.7 %all-gather.13.cloned.1.call-done = bf16[3,1024,512]{1,2,0:T(8,128)(2,1)} async-done(((bf16[3,256,512]{1,2,0:T(8,128)(2,1)}), bf16[3,1024,512]{1,2,0:T(8,128)(2,1)}) %all-gather.13.cloned.1.call-update) | async-done | bytes 3145744 | tf_op jit(solution)/shard_map/all_gather | solution.py:127
  41.9 3.7 convolution_bitcast_fusion
  45.7 1.7 copy-done.23
  48.3 2.2 fusion.20
  52.4 2.3 slice.96
  54.7 39.3 %all-gather.29.cloned.1.call-done = bf16[1,2048,512]{1,2,0:T(8,128)(2,1)} async-done(((bf16[1,512,512]{1,2,0:T(8,128)(2,1)}), bf16[1,2048,512]{1,2,0:T(8,128)(2,1)}) %all-gather.29.cloned.1.call-update) | async-done | bytes 2097168 | tf_op jit(solution)/shard_map/all_gather | solution.py:144
  94.0 16.0 %fusion.1 = (f32[8,512]{1,0:T(8,128)S(1)}, f32[8,512,2048]{2,1,0:T(8,128)}) fusion(pred[512,2048]{1,0:T(8,128)(4,1)S(1)} %broadcast_compare_fusion, bf16[2048,8,64]{0,2,1:T(8,128)(2,1)} %bitcast.209, f32[512,8,64]{0,2,1:T(8,128)} %bitcast.9, f32[8,64]{1,0:T(8,128)S(1)} %add.259), kind=kOutput, calls=%fused_computation.5 | convolution fusion | flops 1099427840 | bytes 37767168 | tf_op jit(solution)/shard_map/qhd,khd->hqk/dot_general | solution.py:156
  110.0 15.1 %exponential_reduce_fusion = f32[8,512]{1,0:T(8,128)S(1)} fusion(f32[8,512,2048]{2,1,0:T(8,128)} %get-tuple-element.96, f32[8,512]{1,0:T(8,128)S(1)} %get-tuple-element.95, pred[512,2048]{1,0:T(8,128)(4,1)S(1)} %broadcast_compare_fusion), kind=kLoop, calls=%fused_computation.2 | loop fusion | flops 33550336 | bytes 34635776 | tf_op jit(solution)/shard_map/reduce_sum | solution.py:173
  125.2 15.5 %all-gather.15.cloned.1.call-done = bf16[2048,1,512]{0,2,1:T(8,128)(2,1)} async-done(((bf16[512,1,512]{0,2,1:T(8,128)(2,1)}), bf16[2048,1,512]{0,2,1:T(8,128)(2,1)}) %all-gather.15.cloned.1.call-update) | async-done | bytes 2097168 | tf_op jit(solution)/shard_map/all_gather | solution.py:145
  140.7 16.4 %fusion.57 = (bf16[512,8,64]{0,2,1:T(8,128)(2,1)S(1)}, f32[512,8,64]{0,2,1:T(8,128)}) fusion(bf16[2048,8,64]{0,2,1:T(8,128)(2,1)} %bitcast.250, f32[8,512,2048]{2,1,0:T(8,128)} %get-tuple-element.96, f32[8,512]{1,0:T(8,128)S(1)} %log_add_fusion, pred[512,2048]{1,0:T(8,128)(4,1)S(1)} %broadcast_compare_fusion), kind=kOutput, calls=%fused_computation.137 | convolution fusion | flops 1107558400 | bytes 38289408 | tf_op jit(solution)/shard_map/hqk,khd->qhd/dot_general | solution.py:176
  158.3 2.9 convolution_convert_fusion.5
  161.3 2.8 convert_element_type.203
  164.2 17.6 %reduce-scatter.11.cloned.1.call-done = bf16[256,1024]{1,0:T(8,128)(2,1)} async-done(((bf16[512,1024]{1,0:T(8,128)(2,1)}), bf16[256,1024]{1,0:T(8,128)(2,1)}) %reduce-scatter.11.cloned.1.call-update) | async-done | bytes 524304 | tf_op jit(solution)/shard_map/reduce_scatter | solution.py:185
  185.8 2.7 convert_element_type.205
  189.0 29.2 %all-gather.21.cloned.1.call-done = bf16[1024,2048]{1,0:T(8,128)(2,1)} async-done(((bf16[256,2048]{1,0:T(8,128)(2,1)}), bf16[1024,2048]{1,0:T(8,128)(2,1)}) %all-gather.21.cloned.1.call-update) | async-done | bytes 4194320 | tf_op jit(solution)/shard_map/all_gather | solution.py:129
  218.3 23.4 %all-gather.19.cloned.1.call-done = bf16[512,1024]{1,0:T(8,128)(2,1)} async-done(((bf16[256,1024]{1,0:T(8,128)(2,1)}), bf16[512,1024]{1,0:T(8,128)(2,1)}) %all-gather.19.cloned.1.call-update) | async-done | bytes 1048592 | tf_op jit(solution)/shard_map/all_gather | solution.py:194
  241.7 7.9 multiply_convert_fusion.1
  249.6 29.3 %all-gather.23.cloned.1.call-done = bf16[2048,1024]{1,0:T(8,128)(2,1)} async-done(((bf16[2048,256]{1,0:T(8,128)(2,1)}), bf16[2048,1024]{1,0:T(8,128)(2,1)}) %all-gather.23.cloned.1.call-update) | async-done | bytes 4194320 | tf_op jit(solution)/shard_map/all_gather | solution.py:130
  278.9 6.1 convolution_convert_fusion.7
  285.1 20.5 %reduce-scatter.13.cloned.1.call-done = bf16[256,1024]{1,0:T(8,128)(2,1)} async-done(((bf16[512,1024]{1,0:T(8,128)(2,1)}), bf16[256,1024]{1,0:T(8,128)(2,1)}) %reduce-scatter.13.cloned.1.call-update) | async-done | bytes 524304 | tf_op jit(solution)/shard_map/reduce_scatter | solution.py:197
  305.6 1.8 fusion.53
  308.2 1.8 fusion.51
  310.0 21.4 %all-gather.25.cloned.1.call-done = bf16[512,1024]{1,0:T(8,128)(2,1)} async-done(((bf16[256,1024]{1,0:T(8,128)(2,1)}), bf16[512,1024]{1,0:T(8,128)(2,1)}) %all-gather.25.cloned.1.call-update) | async-done | bytes 1048592 | tf_op jit(solution)/shard_map/all_gather | solution.py:209
  331.4 7.1 fusion.58
  339.8 3.3 convolution_convert_fusion.6
  343.2 20.5 %reduce-scatter.15.cloned.1.call-done = bf16[256,1024]{1,0:T(8,128)(2,1)} async-done(((bf16[512,1024]{1,0:T(8,128)(2,1)}), bf16[256,1024]{1,0:T(8,128)(2,1)}) %reduce-scatter.15.cloned.1.call-update) | async-done | bytes 524304 | tf_op jit(solution)/shard_map/reduce_scatter | solution.py:214
  363.7 2.8 multiply_reduce_fusion
  369.7 21.2 %all-gather.27.cloned.1.call-done = bf16[512,1024]{1,0:T(8,128)(2,1)} async-done(((bf16[256,1024]{1,0:T(8,128)(2,1)}), bf16[512,1024]{1,0:T(8,128)(2,1)}) %all-gather.27.cloned.1.call-update) | async-done | bytes 1048592 | tf_op jit(solution)/shard_map/all_gather | solution.py:221
  391.0 3.4 multiply_reduce_fusion.1
  394.3 15.3 %convolution_convert_fusion.2 = bf16[8,64,2048]{2,1,0:T(8,128)(2,1)S(1)} fusion(bf16[512,8,64]{0,2,1:T(8,128)(2,1)} %bitcast.215, f32[8,512,2048]{2,1,0:T(8,128)} %get-tuple-element.96, f32[8,512]{1,0:T(8,128)S(1)} %log_add_fusion, pred[512,2048]{1,0:T(8,128)(4,1)S(1)} %broadcast_compare_fusion), kind=kOutput, calls=%fused_computation.22 | convolution fusion | flops 1108344832 | bytes 37240832 | tf_op jit(solution)/shard_map/hqk,qhd->khd/dot_general | solution.py:253
  409.6 2.5 copy.43
  412.2 17.9 %multiply_convert_fusion = bf16[8,512,2048]{2,1,0:T(8,128)(2,1)S(1)} fusion(f32[8,512,2048]{2,1,0:T(8,128)} %get-tuple-element.96, bf16[512,8,64]{0,2,1:T(8,128)(2,1)} %bitcast.216, bf16[2048,8,64]{0,2,1:T(8,128)(2,1)} %bitcast.251, f32[8,512]{1,0:T(8,128)} %bitcast.237, f32[8,512]{1,0:T(8,128)} %copy-done.44, pred[512,2048]{1,0:T(8,128)(4,1)S(1)} %broadcast_compare_fusion), kind=kOutput, calls=%fused_computation | convolution fusion | flops 1132462080 | bytes 54034432 | tf_op jit(solution)/shard_map/qhd,khd->hqk/dot_general | solution.py:240
  430.2 6.8 convolution_convert_fusion.3
  437.0 3.9 copy.42
  442.3 1.7 convolution_convert_fusion.4
  444.3 6.0 convolution_convert_fusion
  452.2 4.4 convolution_convert_fusion.1
  458.2 11.8 %fusion.55 = (f32[8,64]{1,0:T(8,128)S(1)}, bf16[512,8,64]{0,2,1:T(8,128)(2,1)}) fusion(bf16[2048,8,64]{0,2,1:T(8,128)(2,1)S(1)} %bitcast.210, bf16[8,512,2048]{2,1,0:T(8,128)(2,1)} %copy-done), kind=kOutput, calls=%fused_computation.135 | convolution fusion | flops 1074265600 | bytes 19400704 | tf_op jit(solution)/shard_map/hqk,khd->qhd/dot_general | solution.py:243
  471.3 30.2 %reduce-scatter.17.cloned.1.call-done = bf16[512,1,512]{2,0,1:T(8,128)(2,1)} async-done(((bf16[2048,1,512]{2,0,1:T(8,128)(2,1)}), bf16[512,1,512]{2,0,1:T(8,128)(2,1)}) %reduce-scatter.17.cloned.1.call-update) | async-done | bytes 524304 | tf_op jit(solution)/shard_map/reduce_scatter | solution.py:259
  501.5 4.7 convert_bitcast_fusion
  506.2 4.7 copy.47
  512.2 4.7 bitcast_convert_fusion
  516.9 11.5 %reduce-scatter.25.cloned.1.call-done = bf16[512,256]{1,0:T(8,128)(2,1)} async-done(((bf16[512,1024]{1,0:T(8,128)(2,1)}), bf16[512,256]{1,0:T(8,128)(2,1)}) %reduce-scatter.25.cloned.1.call-update) | async-done | bytes 262160 | tf_op jit(solution)/shard_map/reduce_scatter | solution.py:82
  528.5 47.4 %reduce-scatter.29.cloned.1.call-done = bf16[2048,256]{1,0:T(8,128)(2,1)} async-done(((bf16[2048,1024]{1,0:T(8,128)(2,1)}), bf16[2048,256]{1,0:T(8,128)(2,1)}) %reduce-scatter.29.cloned.1.call-update) | async-done | bytes 1048592 | tf_op jit(solution)/shard_map/reduce_scatter | solution.py:88
  575.9 47.6 %reduce-scatter.27.cloned.1.call-done = bf16[256,2048]{1,0:T(8,128)(2,1)} async-done(((bf16[1024,2048]{1,0:T(8,128)(2,1)}), bf16[256,2048]{1,0:T(8,128)(2,1)}) %reduce-scatter.27.cloned.1.call-update) | async-done | bytes 1048592 | tf_op jit(solution)/shard_map/reduce_scatter | solution.py:85
  623.5 2.2 fusion.54
  625.7 1.6 copy.59
  627.3 1.6 copy.60
  629.0 214.1 %all-gather.31.cloned.1.call-done = bf16[12,1024,512]{2,1,0:T(8,128)(2,1)} async-done(((bf16[3,1024,512]{2,1,0:T(8,128)(2,1)}), bf16[12,1024,512]{2,1,0:T(8,128)(2,1)}) %all-gather.31.cloned.1.call-update) | async-done | bytes 12582928 | tf_op jit(solution)/shard_map/all_gather | solution.py:68
  843.1 7.3 reduce_sum.193
  850.4 3.0 copy.58
  854.9 42.3 %all-reduce = (f32[8,1024]{1,0:T(8,128)S(1)}, f32[4096]{0:T(1024)S(1)}) all-reduce(f32[8,1024]{1,0:T(8,128)S(1)} %stack.97, f32[4096]{0:T(1024)S(1)} %dynamic_update_slice.13), channel_id=1, replica_groups=mesh['shard'=4,'context'=4,'tensor'=2] {'shard','context','tensor'}, use_global_device_ids=true, to_apply=%region_33.34 | all-reduce | flops 12288 | bytes 98304 | tf_op jit(solution)/shard_map/psum | solution.py:306
  899.9 2.0 fusion.34
  901.8 61.3 %all-reduce.4.cloned.1.call-done = (bf16[512,256]{1,0:T(8,128)(2,1)}, bf16[256,2048]{1,0:T(8,128)(2,1)}, bf16[2048,256]{1,0:T(8,128)(2,1)}) async-done(((bf16[512,256]{1,0:T(8,128)(2,1)}, bf16[256,2048]{1,0:T(8,128)(2,1)}, bf16[2048,256]{1,0:T(8,128)(2,1)}), (bf16[512,256]{1,0:T(8,128)(2,1)}, bf16[256,2048]{1,0:T(8,128)(2,1)}, bf16[2048,256]{1,0:T(8,128)(2,1)})) %all-reduce.4.cloned.1.call-update) | async-done | bytes 2359312 | tf_op jit(solution)/shard_map/psum | solution.py:71
  967.9 1.7 copy-done.16
  969.6 2.9 fusion.35
  972.5 2.5 pad_maximum_fusion.1
  978.4 2.9 fusion.36
  981.3 2.5 pad_maximum_fusion
  983.7 19.3 %reduce-scatter.23.cloned.1.call-done = bf16[3,256,512]{1,2,0:T(8,128)(2,1)} async-done(((bf16[3,1024,512]{1,2,0:T(8,128)(2,1)}), bf16[3,256,512]{1,2,0:T(8,128)(2,1)}) %reduce-scatter.23.cloned.1.call-update) | async-done | bytes 786448 | tf_op jit(solution)/shard_map/reduce_scatter | solution.py:79
  1003.1 4.0 fusion.28
  1007.3 2.4 copy.55
  1009.7 3.1 copy.54
  (205 shorter events, 36.8 us)
Async XLA Ops:
  7.2 34.7 %all-gather.13.cloned.1.call-start = ((), (), s32[]{:S(2)}) async-start(), calls=%async_computation.10 | async-start | bytes 3932160 | tf_op jit(solution)/shard_map/all_gather | solution.py:127
  9.1 36.5 %copy-start.2 = (f32[3,256,512]{1,2,0:T(8,128)}, f32[3,256,512]{1,2,0:T(8,128)S(1)}, u32[]{:S(2)}) copy-start(f32[3,256,512]{1,2,0:T(8,128)S(1)} %copy.41) | copy-start | bytes 4718596
  9.1 32.8 %copy-start.7 = (bf16[1,512,1024]{2,1,0:T(8,128)(2,1)S(1)}, bf16[1,512,1024]{2,1,0:T(8,128)(2,1)}, u32[]{:S(2)}) copy-start(bf16[1,512,1024]{2,1,0:T(8,128)(2,1)} %param.15) | copy-start | bytes 3145732
  10.1 38.1 %copy-start.35 = (f32[8,1024]{1,0:T(8,128)S(1)}, f32[8,1024]{1,0:T(8,128)}, u32[]{:S(2)}) copy-start(f32[8,1024]{1,0:T(8,128)} %param.22) | copy-start | bytes 98308
  10.1 83.9 %all-gather.29.cloned.1.call-start = ((), (), s32[]{:S(2)}) async-start(), calls=%async_computation.25 | async-start | bytes 2621440 | tf_op jit(solution)/shard_map/all_gather | solution.py:144
  45.7 1.7 copy-start.23
  47.3 3.2 copy-start.25
  48.2 3.6 copy-start.47
  48.2 92.5 %all-gather.15.cloned.1.call-start = ((), (), s32[]{:S(2)}) async-start(), calls=%async_computation.11 | async-start | bytes 2621440 | tf_op jit(solution)/shard_map/all_gather | solution.py:145
  50.5 107.8 %all-gather.17.cloned.1.call-start = ((), (), s32[]{:S(2)}) async-start(), calls=%async_computation.12 | async-start | bytes 1310720 | tf_op jit(solution)/shard_map/all_gather | solution.py:128
  51.3 130.5 %reduce-scatter.11.cloned.1.call-start = ((), (), s32[]{:S(2)}) async-start(), calls=%async_computation.13 | async-start | bytes 1572864 | tf_op jit(solution)/shard_map/reduce_scatter | solution.py:185
  125.2 269.2 %copy-start.44 = (f32[8,512]{1,0:T(8,128)}, f32[8,512]{1,0:T(8,128)S(1)}, u32[]{:S(2)}) copy-start(f32[8,512]{1,0:T(8,128)S(1)} %log_add_fusion) | copy-start | bytes 49156
  157.1 7.0 copy-start.53
  161.3 20.5 %copy-start.8 = (bf16[1,512,1024]{2,1,0:T(8,128)(2,1)S(1)}, bf16[1,512,1024]{2,1,0:T(8,128)(2,1)}, u32[]{:S(2)}) copy-start(bf16[1,512,1024]{2,1,0:T(8,128)(2,1)} %param.15) | copy-start | bytes 3145732
  161.3 57.0 %all-gather.21.cloned.1.call-start = ((), (), s32[]{:S(2)}) async-start(), calls=%async_computation.15 | async-start | bytes 5242880 | tf_op jit(solution)/shard_map/all_gather | solution.py:129
  164.1 77.6 %all-gather.19.cloned.1.call-start = ((), (), s32[]{:S(2)}) async-start(), calls=%async_computation.14 | async-start | bytes 1572864 | tf_op jit(solution)/shard_map/all_gather | solution.py:194
  181.8 2.8 copy-start.1
  185.7 3.3 copy-start.38
  185.7 93.2 %all-gather.23.cloned.1.call-start = ((), (), s32[]{:S(2)}) async-start(), calls=%async_computation.16 | async-start | bytes 5242880 | tf_op jit(solution)/shard_map/all_gather | solution.py:130
  188.4 117.1 %reduce-scatter.13.cloned.1.call-start = ((), (), s32[]{:S(2)}) async-start(), calls=%async_computation.17 | async-start | bytes 1572864 | tf_op jit(solution)/shard_map/reduce_scatter | solution.py:197
  285.0 22.6 %copy-start.19 = (bf16[1,256,1024]{2,1,0:T(8,128)(2,1)S(1)}, bf16[1,256,1024]{2,1,0:T(8,128)(2,1)}, u32[]{:S(2)}) copy-start(bf16[1,256,1024]{2,1,0:T(8,128)(2,1)} %param.17) | copy-start | bytes 1572868
  285.0 46.3 %all-gather.25.cloned.1.call-start = ((), (), s32[]{:S(2)}) async-start(), calls=%async_computation.18 | async-start | bytes 1572864 | tf_op jit(solution)/shard_map/all_gather | solution.py:209
  310.0 53.7 %reduce-scatter.15.cloned.1.call-start = ((), (), s32[]{:S(2)}) async-start(), calls=%async_computation.19 | async-start | bytes 1572864 | tf_op jit(solution)/shard_map/reduce_scatter | solution.py:214
  331.4 8.4 copy-start.49
  339.8 23.9 %copy-start.9 = (bf16[1,512,1024]{2,1,0:T(8,128)(2,1)S(1)}, bf16[1,512,1024]{2,1,0:T(8,128)(2,1)}, u32[]{:S(2)}) copy-start(bf16[1,512,1024]{2,1,0:T(8,128)(2,1)} %param.15) | copy-start | bytes 3145732
  343.1 47.8 %all-gather.27.cloned.1.call-start = ((), (), s32[]{:S(2)}) async-start(), calls=%async_computation.20 | async-start | bytes 1572864 | tf_op jit(solution)/shard_map/all_gather | solution.py:221
  363.7 2.9 copy-start.13
  363.7 2.9 copy-start.27
  367.7 23.3 %copy-start.28 = (bf16[512,1024]{1,0:T(8,128)(2,1)S(1)}, bf16[512,1024]{1,0:T(8,128)(2,1)}, u32[]{:S(2)}) copy-start(bf16[512,1024]{1,0:T(8,128)(2,1)} %all-gather.17.cloned.1.call-done) | copy-start | bytes 3145732
  367.7 23.3 %copy-start.29 = (f32[512,8,64]{0,2,1:T(8,128)S(1)}, f32[512,8,64]{0,2,1:T(8,128)}, u32[]{:S(2)}) copy-start(f32[512,8,64]{0,2,1:T(8,128)} %get-tuple-element.98) | copy-start | bytes 3145732
  369.5 101.7 %reduce-scatter.19.cloned.1.call-start = ((), (), s32[]{:S(2)}) async-start(), calls=%async_computation.22 | async-start | bytes 2621440 | tf_op jit(solution)/shard_map/reduce_scatter | solution.py:262
  412.2 89.4 %reduce-scatter.17.cloned.1.call-start = ((), (), s32[]{:S(2)}) async-start(), calls=%async_computation.21 | async-start | bytes 2621440 | tf_op jit(solution)/shard_map/reduce_scatter | solution.py:259
  430.2 6.8 copy-start
  441.0 3.3 copy-start.51
  441.0 87.5 %reduce-scatter.25.cloned.1.call-start = ((), (), s32[]{:S(2)}) async-start(), calls=%async_computation.27 | async-start | bytes 1310720 | tf_op jit(solution)/shard_map/reduce_scatter | solution.py:82
  444.0 131.9 %reduce-scatter.29.cloned.1.call-start = ((), (), s32[]{:S(2)}) async-start(), calls=%async_computation.29 | async-start | bytes 5242880 | tf_op jit(solution)/shard_map/reduce_scatter | solution.py:88
  450.3 1.9 copy-start.56
  450.3 173.1 %reduce-scatter.27.cloned.1.call-start = ((), (), s32[]{:S(2)}) async-start(), calls=%async_computation.28 | async-start | bytes 5242880 | tf_op jit(solution)/shard_map/reduce_scatter | solution.py:85
  456.6 1.6 copy-start.4
  456.6 44.9 %copy-start.10 = (bf16[1,512,1024]{2,1,0:T(8,128)(2,1)S(1)}, bf16[1,512,1024]{2,1,0:T(8,128)(2,1)}, u32[]{:S(2)}) copy-start(bf16[1,512,1024]{2,1,0:T(8,128)(2,1)} %param.15) | copy-start | bytes 3145732
  456.6 386.4 %all-gather.31.cloned.1.call-start = ((), (), s32[]{:S(2)}) async-start(), calls=%async_computation.26 | async-start | bytes 15728640 | tf_op jit(solution)/shard_map/all_gather | solution.py:68
  511.0 388.9 %reduce-scatter.21.cloned.1.call-start = ((), (), s32[]{:S(2)}) async-start(), calls=%async_computation.23 | async-start | bytes 1572864 | tf_op jit(solution)/shard_map/reduce_scatter | solution.py:273
  516.9 446.3 %all-reduce.4.cloned.1.call-start = ((), (), s32[]{:S(2)}) async-start(), calls=%async_computation.30 | async-start | bytes 4718592 | tf_op jit(solution)/shard_map/psum | solution.py:71
  623.4 379.6 %reduce-scatter.23.cloned.1.call-start = ((), (), s32[]{:S(2)}) async-start(), calls=%async_computation.24 | async-start | bytes 3932160 | tf_op jit(solution)/shard_map/reduce_scatter | solution.py:79
  627.3 1.6 copy-start.20
  853.5 43.8 %copy-start.36 = (f32[8,1024]{1,0:T(8,128)S(1)}, f32[8,1024]{1,0:T(8,128)}, u32[]{:S(2)}) copy-start(f32[8,1024]{1,0:T(8,128)} %param.22) | copy-start | bytes 98308
  853.5 43.8 %copy-start.37 = (f32[2,8,1024]{2,1,0:T(8,128)S(1)}, f32[2,8,1024]{2,1,0:T(8,128)}, u32[]{:S(2)}) copy-start(f32[2,8,1024]{2,1,0:T(8,128)} %param.28) | copy-start | bytes 196612
  853.5 45.1 %copy-start.39 = (f32[4096]{0:T(1024)S(1)}, f32[4096]{0:T(1024)}, u32[]{:S(2)}) copy-start(f32[4096]{0:T(1024)} %param.23) | copy-start | bytes 49156
  853.5 46.4 %copy-start.12 = (f32[256,1024]{1,0:T(8,128)S(1)}, f32[256,1024]{1,0:T(8,128)}, u32[]{:S(2)}) copy-start(f32[256,1024]{1,0:T(8,128)} %copy-done.11) | copy-start | bytes 3145732
  854.2 109.0 %copy-start.22 = (f32[2,512,256]{2,1,0:T(8,128)S(1)}, f32[2,512,256]{2,1,0:T(8,128)}, u32[]{:S(2)}) copy-start(f32[2,512,256]{2,1,0:T(8,128)} %param.25) | copy-start | bytes 3145732
  897.2 67.0 %copy-start.40 = (f32[8,1024]{1,0:T(8,128)}, f32[8,1024]{1,0:T(8,128)S(1)}, u32[]{:S(2)}) copy-start(f32[8,1024]{1,0:T(8,128)S(1)} %get-tuple-element.48) | copy-start | bytes 98308
  897.2 67.0 %copy-start.45 = (f32[4096]{0:T(1024)}, f32[4096]{0:T(1024)S(1)}, u32[]{:S(2)}) copy-start(f32[4096]{0:T(1024)S(1)} %get-tuple-element.49) | copy-start | bytes 49156
  898.6 65.7 %copy-start.26 = (f32[512,256]{1,0:T(8,128)S(1)}, f32[512,256]{1,0:T(8,128)}, u32[]{:S(2)}) copy-start(f32[512,256]{1,0:T(8,128)} %param.19) | copy-start | bytes 1572868
  964.2 2.3 copy-start.24
  964.3 2.9 copy-start.5
  964.3 3.2 copy-start.31
  967.5 2.1 copy-start.16
  967.9 4.6 copy-start.14
  972.5 4.0 copy-start.6
  972.5 4.3 copy-start.30
  977.5 3.8 copy-start.15
  981.3 21.8 %copy-start.3 = (f32[3,256,512]{1,2,0:T(8,128)S(1)}, f32[3,256,512]{1,2,0:T(8,128)}, u32[]{:S(2)}) copy-start(f32[3,256,512]{1,2,0:T(8,128)} %copy-done.2) | copy-start | bytes 4718596
  981.3 21.8 %copy-start.18 = (f32[1,3,256,512]{2,3,1,0:T(8,128)S(1)}, f32[1,3,256,512]{2,3,1,0:T(8,128)}, u32[]{:S(2)}) copy-start(f32[1,3,256,512]{2,3,1,0:T(8,128)} %copy.59) | copy-start | bytes 4718596
  1009.7 3.1 copy-start.21
  (14 other events, 16.9 us)
Sparse Core Ops, SparseCore 0:
  10.2 31.6 all-gather.12
  48.3 45.6 all-gather.28
  96.2 44.4 all-gather.14
  142.7 15.6 all-gather.16
  161.4 20.3 reduce-scatter.10
  183.8 34.4 all-gather.20
  220.4 21.2 all-gather.18
  243.8 34.9 all-gather.22
  285.1 20.3 reduce-scatter.12
  310.1 21.2 all-gather.24
  343.3 20.3 reduce-scatter.14
  369.6 21.2 all-gather.26
  412.3 43.6 reduce-scatter.18
  458.7 42.8 reduce-scatter.16
  504.5 23.9 reduce-scatter.24
  531.4 44.3 reduce-scatter.28
  578.8 44.5 reduce-scatter.26
  624.8 218.1 all-gather.30
  845.9 19.0 reduce-scatter.20
  867.4 95.6 all-reduce.3
  966.3 36.7 reduce-scatter.22
